TPU v7x, 32 devices: a whole 2x2x4 slice. The times are simulated.
32 devices in a mesh: section: 2 (over core), ctx: 4 (over z), mp: 4 (over y, x).
Axes of the slice: x: 2, y: 2, z: 4, core: 2. Of those that a mesh axis runs over, the one named last changes fastest.
Arguments:
- frames: bfloat16 [2, 16, 128, 512], P('section', 'ctx'), may hold values from -6 to 6
- w_conv: bfloat16 [3, 512, 512], replicated, may hold values from -0.15625 to 0.15625
- w_lat: bfloat16 [512, 16], replicated, may hold values from -0.25 to 0.25
- dest: int32 [2, 512, 1], P(None, 'ctx'), may hold values from 0 to 3; in each aligned block of 128 rows (0 to 127, 128 to 255, ..., all dimensions but the last counted through in order) at most 48 rows name the same one
- pick: int32 [2, 512], P(None, 'ctx'), may hold values from 0 to 6
- w_embed: bfloat16 [64, 6144], replicated, may hold values from -0.75 to 0.75
- gain: float32 [6144], replicated, may hold values from 0.25 to 1.75
- w_qkv: bfloat16 [6144, 3, 4096], P(None, None, 'mp'), may hold values from -0.078125 to 0.078125
Outputs:
- attended: bfloat16 [2, 768, 4096], P('section', 'ctx', 'mp')
Inputs may be any that keep to these rules, and one draw needn't show every extreme that they name: `dest`: among the 128 rows of one frame block, at most 48 name the same context shard, and some frame block reaches 48.
All inputs are finite; a program needn't handle non-finite values.
Results may differ from a plain program's by a relative error of at most 0.0061.
Values may be sent and summed in bfloat16 or wider, within the bound.
A program may use at most 128 MiB of HBM per device.

v0:
```python
import jax
import jax.numpy as jnp
from jax import lax
from jax.sharding import PartitionSpec as P

HEAD = 128
GROUP = 4


def partner(block, axis, distance):
    count = lax.axis_size(axis)
    route = []
    for low in range(count):
        high = low | 1 << distance
        if high != low and high < count:
            route += [(low, high), (high, low)]
    return lax.ppermute(block, axis, route)


def encode(frame_block, w_conv, w_lat):
    frame_count = frame_block.shape[0]
    cells_here = frame_block.shape[1]
    channels = frame_block.shape[2]
    empty_frame = jnp.zeros_like(frame_block[:1])
    back_one = jnp.concatenate([empty_frame, frame_block[:-1]], axis=0)
    back_two = jnp.concatenate([empty_frame, empty_frame, frame_block[:-2]], axis=0)
    hidden = jnp.dot(
        frame_block.reshape(-1, channels), w_conv[0], preferred_element_type=jnp.float32
    )
    hidden = hidden + jnp.dot(
        back_one.reshape(-1, channels), w_conv[1], preferred_element_type=jnp.float32
    )
    hidden = hidden + jnp.dot(
        back_two.reshape(-1, channels), w_conv[2], preferred_element_type=jnp.float32
    )
    active = jax.nn.silu(hidden).astype(jnp.bfloat16)
    latent = jnp.dot(active, w_lat, preferred_element_type=jnp.float32).astype(jnp.bfloat16)
    return latent.reshape(frame_count, cells_here // 4, 4 * w_lat.shape[1])


def head_norm(values):
    return values * lax.rsqrt(jnp.mean(values * values, axis=-1, keepdims=True) + 1e-06)


def on_device(frames, w_conv, w_lat, dest, pick, w_embed, gain, w_qkv):
    frame_block = frames[0]
    patch_grid = encode(frame_block, w_conv, w_lat)
    patch_rows = patch_grid.reshape(-1, patch_grid.shape[-1])
    arrived = partner(patch_rows, "section", 0)
    shard_count = lax.axis_size("ctx")
    row_count = arrived.shape[0]
    source = 1 - lax.axis_index("section")
    targets = lax.dynamic_index_in_dim(dest[:, :, 0], source, 0, keepdims=False)
    choose = lax.dynamic_index_in_dim(pick, source, 0, keepdims=False)
    tier = (choose >= 4).astype(jnp.int32) + (choose >= 6).astype(jnp.int32)
    labels = targets // GROUP + shard_count // GROUP * tier + 1
    onehot = (targets[:, None] == jnp.arange(shard_count, dtype=jnp.int32)[None, :]).astype(
        jnp.int32
    )
    before = jnp.cumsum(onehot, axis=0, dtype=jnp.int32) - onehot
    within = jnp.sum(before * onehot, axis=1, dtype=jnp.int32)
    capacity = max(2, 3 * row_count // (2 * shard_count))
    position = targets * capacity + within
    outgoing = (
        jnp.zeros((shard_count * capacity, arrived.shape[1]), jnp.bfloat16)
        .at[position]
        .set(arrived)
    )
    outgoing = outgoing.reshape(shard_count, capacity, arrived.shape[1])
    out_labels = jnp.zeros((shard_count * capacity,), jnp.int32).at[position].set(labels)
    out_labels = out_labels.reshape(shard_count, capacity)
    incoming, in_labels = (
        lax.all_to_all(outgoing, "ctx", split_axis=0, concat_axis=0, tiled=True),
        lax.all_to_all(out_labels, "ctx", split_axis=0, concat_axis=0, tiled=True),
    )
    packed = incoming.reshape(-1, incoming.shape[-1])
    owners = in_labels.reshape(-1)
    embedded = jnp.dot(packed, w_embed, preferred_element_type=jnp.float32)
    normed = (
        embedded * lax.rsqrt(jnp.mean(embedded * embedded, axis=-1, keepdims=True) + 1e-06) * gain
    ).astype(jnp.bfloat16)
    heads_here = w_qkv.shape[2] // HEAD
    projected = jnp.dot(
        normed, w_qkv.reshape(w_qkv.shape[0], -1), preferred_element_type=jnp.float32
    )
    projected = projected.reshape(-1, 3, heads_here, HEAD)
    queries = head_norm(projected[:, 0]).astype(jnp.bfloat16)
    keys_own = head_norm(projected[:, 1]).astype(jnp.bfloat16)
    values_own = projected[:, 2].astype(jnp.bfloat16)
    factor = 1.0 / HEAD**0.5
    key_piece = lax.all_gather(keys_own, "ctx", axis=0, tiled=True)
    value_piece = lax.all_gather(values_own, "ctx", axis=0, tiled=True)
    label_piece = lax.all_gather(owners, "ctx", axis=0, tiled=True)
    scores = (
        jnp.einsum("qhd,khd->hqk", queries, key_piece, preferred_element_type=jnp.float32) * factor
    )
    allowed = (owners[:, None] == label_piece[None, :]) & (owners[:, None] > 0)
    expo = jnp.where(allowed[None], jnp.exp(scores), 0.0)
    total = jnp.sum(expo, axis=-1).T
    summed = jnp.einsum(
        "hqk,khd->qhd", expo.astype(jnp.bfloat16), value_piece, preferred_element_type=jnp.float32
    )
    summed, total = (summed, total)
    empty_slot = (owners == 0).astype(jnp.float32)
    attended = summed / (total + empty_slot[:, None])[:, :, None]
    return attended.reshape(1, queries.shape[0], heads_here * HEAD).astype(jnp.bfloat16)


def solution(mesh):
    in_specs = (
        P("section", "ctx", None, None),
        P(),
        P(),
        P(None, "ctx", None),
        P(None, "ctx"),
        P(),
        P(),
        P(None, None, "mp"),
    )
    out_specs = P("section", "ctx", "mp")
    return jax.shard_map(
        on_device, mesh=mesh, in_specs=in_specs, out_specs=out_specs, check_vma=False
    )
```

profile of v0, /device:TPU:0, one launch (start us, length us, event | category | flops | bytes accessed | tf_op | source)
XLA Modules:
  0.0 183.4 jit_solution(528463704101767966)
XLA Ops:
  6.5 1.2 slice_bitcast_fusion.2
  7.7 1.0 slice_bitcast_fusion.3
  8.7 0.8 concatenate.8
  9.6 1.6 fusion.31
  11.2 0.0 copy-done.2
  11.2 0.0 copy-start.3
  11.2 0.4 convolution_add_fusion.1
  11.7 1.8 convolution_convert_fusion
  13.5 0.1 copy.9
  13.6 0.1 reshape_reshape.3
  13.8 0.6 collective-permute-start
  14.3 0.1 fusion.40
  14.4 0.2 reduce_window_sum.11
  14.6 0.2 select_reduce_fusion
  14.8 0.4 collective-permute-done
  15.2 0.9 scatter_custom_fusion
  16.1 0.7 reshape.205
  16.8 6.2 %all-to-all-start = ((bf16[4,2,1536]{2,1,0:T(2,128)(2,1)}), bf16[4,2,1536]{2,1,0:T(2,128)(2,1)S(1)}, u32[]{:S(2)}, u32[]{:S(2)}) async-start(bf16[4,2,1536]{2,1,0:T(2,128)(2,1)} %reshape.205), calls=%async_computation | async-start | bytes 49152 | tf_op jit(solution)/shard_map/all_to_all | solution.py:73
  23.0 0.0 all-gather.4.cloned.1.call-start
  23.0 48.7 %copy.10 = bf16[6144,3,1024]{0,2,1:T(8,128)(2,1)} copy(bf16[6144,3,1024]{2,0,1:T(8,128)(2,1)} %param.15) | data formatting | bytes 75497472 | tf_op args[7]
  71.7 0.0 all-to-all-done
  71.7 0.1 reshape.206
  71.8 2.9 %multiply_reduce_fusion = (f32[192]{0:T(256)S(1)}, f32[192,6144]{1,0:T(8,128)}) fusion(bf16[192,64]{1,0:T(8,128)(2,1)S(1)} %bitcast.92, bf16[64,6144]{1,0:T(8,128)(2,1)S(1)} %copy-done), kind=kOutput, calls=%fused_computation.4 | convolution fusion | flops 153354048 | bytes 5530368 | tf_op jit(solution)/shard_map/dot_general | solution.py:78
  74.7 0.0 copy-start.7
  74.7 18.8 %fusion.5 = f32[192,3,8,128]{3,0,2,1:T(8,128)S(1)} fusion(bf16[3,8,128,6144]{3,2,1,0:T(8,128)(2,1)} %bitcast.88, f32[192,6144]{1,0:T(8,128)} %get-tuple-element.10, f32[6144]{0:T(1024)S(1)} %copy-done.5, f32[192]{0:T(256)S(1)} %add_rsqrt_fusion.2), kind=kOutput, calls=%fused_computation.9 | convolution fusion | flops 7251296256 | bytes 44851968 | tf_op jit(solution)/shard_map/dot_general | solution.py:83
  93.5 0.6 multiply_reduce_fusion.2
  94.2 1.0 multiply_convert_fusion.2
  95.2 0.0 all-gather.4.cloned.1.call-update
  95.2 0.0 all-gather.6.cloned.1.call-start
  95.3 0.8 slice.71
  96.1 0.0 all-gather.6.cloned.1.call-update
  96.1 1.0 scatter_custom_fusion.1
  97.1 0.7 all_to_all.10
  97.8 5.1 %all-to-all-start.1 = ((s32[4,1,48]{2,1,0:T(1,128)}), s32[4,1,48]{2,1,0:T(1,128)S(1)}, u32[]{:S(2)}, u32[]{:S(2)}) async-start(s32[4,1,48]{2,1,0:T(1,128)} %all_to_all.10), calls=%async_computation.1 | async-start | bytes 4096 | tf_op jit(solution)/shard_map/all_to_all | solution.py:74
  102.9 0.6 dynamic-slice.1
  104.1 4.3 %all-to-all-done.1 = s32[4,1,48]{2,1,0:T(1,128)S(1)} async-done(((s32[4,1,48]{2,1,0:T(1,128)}), s32[4,1,48]{2,1,0:T(1,128)S(1)}, u32[]{:S(2)}, u32[]{:S(2)}) %all-to-all-start.1) | async-done | bytes 800 | tf_op jit(solution)/shard_map/all_to_all | solution.py:74
  108.4 0.6 broadcast.155
  109.0 0.6 reduce.3
  109.6 0.1 reshape.186
  109.7 0.2 dynamic-update-slice
  109.9 7.0 %all-reduce.2 = s32[768]{0:T(1024)S(1)} all-reduce(s32[768]{0:T(1024)S(1)} %dynamic-update-slice), channel_id=1, replica_groups=mesh['section'=2,'ctx'=4,'mp'=4] {'ctx'}, use_global_device_ids=true, to_apply=%add.2 | all-reduce | flops 768 | bytes 6144
  116.9 0.2 compare_and_fusion
  117.1 16.9 %all-gather.4.cloned.1.call-done = bf16[768,8,128]{2,0,1:T(8,128)(2,1)} async-done(((bf16[192,8,128]{2,0,1:T(8,128)(2,1)}), bf16[768,8,128]{2,0,1:T(8,128)(2,1)}) %all-gather.4.cloned.1.call-update) | async-done | bytes 1572880 | tf_op jit(solution)/shard_map/all_gather | solution.py:91
  134.1 4.8 %fusion = (f32[8,192]{1,0:T(8,128)S(1)}, f32[8,192,768]{2,1,0:T(8,128)}) fusion(pred[192,768]{1,0:T(8,128)(4,1)S(1)} %compare_and_fusion, bf16[768,8,128]{2,0,1:T(8,128)(2,1)} %all-gather.4.cloned.1.call-done, f32[192,3,8,128]{3,0,2,1:T(8,128)S(1)} %fusion.5, f32[192,8]{0,1:T(8,128)S(1)} %add_rsqrt_fusion.1), kind=kOutput, calls=%fused_computation.5 | convolution fusion | flops 305920512 | bytes 7239680 | tf_op jit(solution)/shard_map/qhd,khd->hqk/dot_general | solution.py:95
  138.9 32.6 %all-gather.6.cloned.1.call-done = bf16[768,1,8,128]{3,0,2,1:T(8,128)(2,1)} async-done(((bf16[192,1,8,128]{3,0,2,1:T(8,128)(2,1)}), bf16[768,1,8,128]{3,0,2,1:T(8,128)(2,1)}) %all-gather.6.cloned.1.call-update) | async-done | bytes 1572880 | tf_op jit(solution)/shard_map/all_gather | solution.py:92
  171.5 3.8 %fusion.23 = bf16[192,8,128]{2,0,1:T(8,128)(2,1)S(1)} fusion(bf16[768,1,8,128]{3,0,2,1:T(8,128)(2,1)} %all-gather.6.cloned.1.call-done, f32[8,192,768]{2,1,0:T(8,128)} %get-tuple-element.12, pred[192,768]{1,0:T(8,128)(4,1)S(1)} %compare_and_fusion, f32[192,8]{0,1:T(8,128)S(1)} %add_bitcast_fusion), kind=kOutput, calls=%fused_computation.22 | convolution fusion | flops 305922048 | bytes 6838272 | tf_op jit(solution)/shard_map/hqk,khd->qhd/dot_general | solution.py:100
  175.4 0.3 copy.11
  175.6 0.9 convert_element_type.66
  (23 shorter events, 0.1 us)
Async XLA Ops:
  6.5 65.3 %copy-start = (bf16[64,6144]{1,0:T(8,128)(2,1)S(1)}, bf16[64,6144]{1,0:T(8,128)(2,1)}, u32[]{:S(2)}) copy-start(bf16[64,6144]{1,0:T(8,128)(2,1)} %param.13) | copy-start | bytes 2359300
  6.5 4.7 %copy-start.2 = (bf16[3,512,512]{2,1,0:T(8,128)(2,1)S(1)}, bf16[3,512,512]{2,1,0:T(8,128)(2,1)}, u32[]{:S(2)}) copy-start(bf16[3,512,512]{2,1,0:T(8,128)(2,1)} %param.9) | copy-start | bytes 4718596
  6.5 5.1 %copy-start.6 = (bf16[512,16]{0,1:T(8,128)(2,1)S(1)}, bf16[512,16]{0,1:T(8,128)(2,1)}, u32[]{:S(2)}) copy-start(bf16[512,16]{0,1:T(8,128)(2,1)} %param.10) | copy-start | bytes 49156
  11.2 3.1 %copy-start.3 = (s32[2,128,1]{1,2,0:T(1,128)S(1)}, s32[2,128,1]{1,2,0:T(1,128)}, u32[]{:S(2)}) copy-start(s32[2,128,1]{1,2,0:T(1,128)} %param.11) | copy-start | bytes 3076
  13.8 1.4 collective-permute-start
  16.8 54.9 %all-to-all-start = ((bf16[4,2,1536]{2,1,0:T(2,128)(2,1)}), bf16[4,2,1536]{2,1,0:T(2,128)(2,1)S(1)}, u32[]{:S(2)}, u32[]{:S(2)}) async-start(bf16[4,2,1536]{2,1,0:T(2,128)(2,1)} %reshape.205), calls=%async_computation | async-start | bytes 49152 | tf_op jit(solution)/shard_map/all_to_all | solution.py:73
  23.0 111.1 %all-gather.4.cloned.1.call-start = ((), (), s32[]{:S(2)}) async-start(), calls=%async_computation.2 | async-start | bytes 1966080 | tf_op jit(solution)/shard_map/all_gather | solution.py:91
  71.7 3.0 %copy-start.5 = (f32[6144]{0:T(1024)S(1)}, f32[6144]{0:T(1024)}, u32[]{:S(2)}) copy-start(f32[6144]{0:T(1024)} %param.14) | copy-start | bytes 73732
  74.7 21.4 %copy-start.4 = (s32[2,128]{1,0:T(2,128)S(1)}, s32[2,128]{1,0:T(2,128)}, u32[]{:S(2)}) copy-start(s32[2,128]{1,0:T(2,128)} %param.12) | copy-start | bytes 3076
  74.7 28.1 %copy-start.7 = (u32[32]{0:T(128)S(1)}, u32[32]{0:T(128)}, u32[]{:S(2)}) copy-start(u32[32]{0:T(128)} %constant.76) | copy-start | bytes 388
  95.2 76.3 %all-gather.6.cloned.1.call-start = ((), (), s32[]{:S(2)}) async-start(), calls=%async_computation.3 | async-start | bytes 1966080 | tf_op jit(solution)/shard_map/all_gather | solution.py:92
  97.8 10.6 %all-to-all-start.1 = ((s32[4,1,48]{2,1,0:T(1,128)}), s32[4,1,48]{2,1,0:T(1,128)S(1)}, u32[]{:S(2)}, u32[]{:S(2)}) async-start(s32[4,1,48]{2,1,0:T(1,128)} %all_to_all.10), calls=%async_computation.1 | async-start | bytes 4096 | tf_op jit(solution)/shard_map/all_to_all | solution.py:74
  171.5 5.0 %copy-start.1 = (bf16[64,6144]{1,0:T(8,128)(2,1)S(1)}, bf16[64,6144]{1,0:T(8,128)(2,1)}, u32[]{:S(2)}) copy-start(bf16[64,6144]{1,0:T(8,128)(2,1)} %param.13) | copy-start | bytes 2359300
Sparse Core Ops, SparseCore 0:
  95.3 38.6 all-gather.3
  135.6 35.8 all-gather.5
where the time goes:
time: 185 us; the launch traced here: 183 us
  local copies, waits for them, and re-layouts  58.8 us (32%)
  waiting for transfers between devices  54.3 us (29%)
  matrix products  34.2 us (18%)
  between operations  14.2 us (8%)
  starting transfers between devices  11.9 us (6%)
  blocking collectives  7.03 us (4%)
  other arithmetic  2.93 us (2%)
    unnamed x22, local copies, waits for them, and re-layouts  50.4 us
    all_gather x1, waiting for transfers between devices, on_device(): value_piece = lax.all_gather(values_own, 'ctx', axis=0, tiled=True)  32.6 us
    dot_general x1, matrix products, on_device(): jnp.dot(normed, w_qkv.reshape(w_qkv.shape[0], -1), preferred_element_type...  18.8 us
    all_gather x1, waiting for transfers between devices, on_device(): key_piece = lax.all_gather(keys_own, 'ctx', axis=0, tiled=True)  16.9 us
    unnamed x1, blocking collectives  7.03 us
    all_to_all x1, starting transfers between devices, on_device(): lax.all_to_all(outgoing, 'ctx', split_axis=0, concat_axis=0, tiled=True)  6.2 us
    all_to_all x1, starting transfers between devices, on_device(): lax.all_to_all(out_labels, 'ctx', split_axis=0, concat_axis=0, tiled=True)  5.09 us
    dot_general x1, matrix products, on_device(): jnp.einsum('qhd,khd->hqk', queries, key_piece, preferred_element_type=jnp...  4.84 us
  transfers between devices with their start and end apart: 5, of which 4 were waited for; matrix products, arithmetic and copies ran while one was open for 32% of the time, Pallas kernels for 0%

commit v1 on v0

--- a/solution.py
+++ b/solution.py
@@ -5,6 +5,20 @@
 
 HEAD = 128
 GROUP = 4
+
+
+def ring_apply(shard, axis, dim, make, out_dim):
+    ways, here, step = (lax.axis_size(axis), lax.axis_index(axis), shard.shape[dim])
+    earlier, later = ([], [])
+    going_up = going_down = shard
+    for far in range(ways // 2 + 1):
+        earlier.append(make(going_up, (here - far) % ways * step))
+        if 0 < far < ways - ways // 2:
+            later.append(make(going_down, (here + far) % ways * step))
+        going_up = lax.ppermute(going_up, axis, [(d, (d + 1) % ways) for d in range(ways)])
+        going_down = lax.ppermute(going_down, axis, [(d, (d - 1) % ways) for d in range(ways)])
+    line = jnp.concatenate([*earlier[::-1], *later], axis=out_dim)
+    return jnp.roll(line, (here - ways // 2) * earlier[0].shape[out_dim], axis=out_dim)
 
 
 def partner(block, axis, distance):
@@ -88,11 +102,19 @@
     keys_own = head_norm(projected[:, 1]).astype(jnp.bfloat16)
     values_own = projected[:, 2].astype(jnp.bfloat16)
     factor = 1.0 / HEAD**0.5
-    key_piece = lax.all_gather(keys_own, "ctx", axis=0, tiled=True)
     value_piece = lax.all_gather(values_own, "ctx", axis=0, tiled=True)
     label_piece = lax.all_gather(owners, "ctx", axis=0, tiled=True)
     scores = (
-        jnp.einsum("qhd,khd->hqk", queries, key_piece, preferred_element_type=jnp.float32) * factor
+        ring_apply(
+            keys_own,
+            "ctx",
+            0,
+            lambda part, at: jnp.einsum(
+                "qhd,khd->hqk", queries, part, preferred_element_type=jnp.float32
+            ),
+            2,
+        )
+        * factor
     )
     allowed = (owners[:, None] == label_piece[None, :]) & (owners[:, None] > 0)
     expo = jnp.where(allowed[None], jnp.exp(scores), 0.0)

time: 185 us -> 194 us (1.049)
  waiting for transfers between devices: 54.3 us -> 38.4 us
  local copies, waits for them, and re-layouts: 58.8 us -> 71.6 us
  starting transfers between devices: 11.9 us -> 16.4 us
  other arithmetic: 2.93 us -> 6.95 us
    ppermute x0 -> x3, waiting for transfers between devices: none -> 38.4 us  [the longest x1 20.4 us: ring_apply(): lax.ppermute(going_down, axis, [(d, (d - 1) % ways) for d in range(ways)])]
    all_gather x1, waiting for transfers between devices: 32.6 us -> 0.02 us  [on_device(): value_piece = lax.all_gather(values_own, 'ctx', axis=0, tiled=True)]
    all_gather x1 -> x0, waiting for transfers between devices: 16.9 us -> none  [on_device(): key_piece = lax.all_gather(keys_own, 'ctx', axis=0, tiled=True)]
    concatenate x0 -> x1, local copies, waits for them, and re-layouts: none -> 12.8 us  [ring_apply(): jnp.roll(line, (here - ways // 2) * earlier[0].shape[out_dim], axis=out_dim)]
    ppermute x0 -> x3, starting transfers between devices: none -> 4.82 us  [the longest x2 2.42 us: ring_apply(): lax.ppermute(going_up, axis, [(d, (d + 1) % ways) for d in range(ways)])]
    reduce_sum x0 -> x1, other arithmetic: none -> 4.53 us  [on_device(): total = jnp.sum(expo, axis=-1).T]
    all_to_all x1, waiting for transfers between devices: 4.3 us -> 0.01 us  [on_device(): lax.all_to_all(out_labels, 'ctx', split_axis=0, concat_axis=0, tiled=True)]
    dot_general x1 -> x4, matrix products: 4.84 us -> 5 us  [on_device(): jnp.einsum('qhd,khd->hqk', queries, part, preferred_element_type=jnp.floa...]
  transfers between devices with their start and end apart: 5 -> 7, of which waited for: 4 -> 3; matrix products, arithmetic and copies ran while one was open for 32% -> 39% of each run, Pallas kernels for 0% -> 0%
where the time goes in v1:
time: 194 us; the launch traced here: 192 us
  local copies, waits for them, and re-layouts  71.6 us (37%)
  waiting for transfers between devices  38.4 us (20%)
  matrix products  35.2 us (18%)
  starting transfers between devices  16.4 us (8%)
  between operations  14.3 us (7%)
  blocking collectives  8.78 us (5%)
  other arithmetic  6.95 us (4%)
    unnamed x22, local copies, waits for them, and re-layouts  50.4 us
    ppermute x1, waiting for transfers between devices, ring_apply(): lax.ppermute(going_down, axis, [(d, (d - 1) % ways) for d in range(ways)])  20.4 us
    dot_general x1, matrix products, on_device(): jnp.dot(normed, w_qkv.reshape(w_qkv.shape[0], -1), preferred_element_type...  18.8 us
    ppermute x2, waiting for transfers between devices, ring_apply(): lax.ppermute(going_up, axis, [(d, (d + 1) % ways) for d in range(ways)])  17.9 us
    concatenate x1, local copies, waits for them, and re-layouts, ring_apply(): jnp.roll(line, (here - ways // 2) * earlier[0].shape[out_dim], axis=out_dim)  12.8 us
    unnamed x1, blocking collectives  8.78 us
    all_to_all x1, starting transfers between devices, on_device(): lax.all_to_all(out_labels, 'ctx', split_axis=0, concat_axis=0, tiled=True)  5.89 us
    all_to_all x1, starting transfers between devices, on_device(): lax.all_to_all(outgoing, 'ctx', split_axis=0, concat_axis=0, tiled=True)  5.09 us
  transfers between devices with their start and end apart: 7, of which 3 were waited for; matrix products, arithmetic and copies ran while one was open for 39% of the time, Pallas kernels for 0%

profile of v1, /device:TPU:0, one launch (start us, length us, event | category | flops | bytes accessed | tf_op | source)
XLA Modules:
  0.0 191.5 jit_solution(10187147720428830437)
XLA Ops:
  6.5 1.2 slice_bitcast_fusion.2
  7.7 1.0 slice_bitcast_fusion.3
  8.7 0.8 concatenate.14
  9.6 1.6 fusion.31
  11.2 0.4 convolution_add_fusion.1
  11.7 1.8 convolution_convert_fusion
  13.5 0.1 copy.9
  13.6 0.1 reshape_reshape.3
  13.8 0.6 collective-permute-start
  14.3 0.1 fusion.38
  14.4 0.2 reduce_window_sum.11
  14.6 0.2 select_reduce_fusion
  14.8 1.0 scatter_custom_fusion.1
  15.8 0.7 all_to_all.10
  16.5 5.9 %all-to-all-start.1 = ((s32[4,1,48]{2,1,0:T(1,128)}), s32[4,1,48]{2,1,0:T(1,128)S(1)}, u32[]{:S(2)}, u32[]{:S(2)}) async-start(s32[4,1,48]{2,1,0:T(1,128)} %all_to_all.10), calls=%async_computation.1 | async-start | bytes 4096 | tf_op jit(solution)/shard_map/all_to_all | solution.py:88
  22.4 48.7 %copy.10 = bf16[6144,3,1024]{0,2,1:T(8,128)(2,1)} copy(bf16[6144,3,1024]{2,0,1:T(8,128)(2,1)} %param.15) | data formatting | bytes 75497472 | tf_op args[7]
  71.1 0.6 dynamic-slice.1
  72.3 0.5 broadcast.155
  72.8 0.7 reduce.3
  73.5 0.1 reshape.186
  73.6 0.9 scatter_custom_fusion
  74.5 0.7 reshape.205
  75.2 5.1 %all-to-all-start = ((bf16[4,2,1536]{2,1,0:T(2,128)(2,1)}), bf16[4,2,1536]{2,1,0:T(2,128)(2,1)S(1)}, u32[]{:S(2)}, u32[]{:S(2)}) async-start(bf16[4,2,1536]{2,1,0:T(2,128)(2,1)} %reshape.205), calls=%async_computation | async-start | bytes 49152 | tf_op jit(solution)/shard_map/all_to_all | solution.py:87
  80.3 0.2 dynamic-update-slice
  80.6 8.8 %all-reduce.2 = s32[768]{0:T(1024)S(1)} all-reduce(s32[768]{0:T(1024)S(1)} %dynamic-update-slice), channel_id=1, replica_groups=mesh['section'=2,'ctx'=4,'mp'=4] {'ctx'}, use_global_device_ids=true, to_apply=%add.2 | all-reduce | flops 768 | bytes 6144
  89.3 0.1 reshape.206
  89.5 2.9 %multiply_reduce_fusion = (f32[192]{0:T(256)S(1)}, f32[192,6144]{1,0:T(8,128)}) fusion(bf16[192,64]{1,0:T(8,128)(2,1)S(1)} %bitcast.96, bf16[64,6144]{1,0:T(8,128)(2,1)S(1)} %copy-done), kind=kOutput, calls=%fused_computation.4 | convolution fusion | flops 153354048 | bytes 5530368 | tf_op jit(solution)/shard_map/dot_general | solution.py:92
  92.4 18.8 %fusion.5 = f32[192,3,8,128]{3,0,2,1:T(8,128)S(1)} fusion(bf16[3,8,128,6144]{3,2,1,0:T(8,128)(2,1)} %bitcast.92, f32[192,6144]{1,0:T(8,128)} %get-tuple-element.12, f32[6144]{0:T(1024)S(1)} %copy-done.5, f32[192]{0:T(256)S(1)} %add_rsqrt_fusion.2), kind=kOutput, calls=%fused_computation.9 | convolution fusion | flops 7251296256 | bytes 44851968 | tf_op jit(solution)/shard_map/dot_general | solution.py:97
  111.2 0.6 multiply_reduce_fusion.1
  111.8 0.8 slice.70
  112.6 0.5 multiply_convert_fusion.2
  113.1 1.5 collective-permute-start.1
  114.6 0.2 compare_and_fusion
  114.8 2.4 %collective-permute-start.3 = (bf16[192,8,128]{2,0,1:T(8,128)(2,1)S(1)}, bf16[192,8,128]{2,0,1:T(8,128)(2,1)S(1)}, u32[]{:S(2)}, u32[]{:S(2)}) collective-permute-start(bf16[192,8,128]{2,0,1:T(8,128)(2,1)S(1)} %get-tuple-element.7), channel_id=1, source_target_pairs={{0,12},{4,0},{8,4},{12,8},{1,13},{5,1},{9,5},{13,9},{2,14},{6,2},{... | collective-permute-start | bytes 1179656 | tf_op jit(solution)/shard_map/ppermute | solution.py:19
  117.2 0.4 fusion.55
  117.6 12.2 %collective-permute-done.1 = bf16[192,8,128]{2,0,1:T(8,128)(2,1)S(1)} collective-permute-done((bf16[192,8,128]{2,0,1:T(8,128)(2,1)S(1)}, bf16[192,8,128]{2,0,1:T(8,128)(2,1)S(1)}, u32[]{:S(2)}, u32[]{:S(2)}) %collective-permute-start.1) | collective-permute-done | bytes 393248 | tf_op jit(solution)/shard_map/ppermute | solution.py:18
  129.8 0.9 collective-permute-start.2
  130.7 1.6 fusion.54
  132.3 20.4 %collective-permute-done.3 = bf16[192,8,128]{2,0,1:T(8,128)(2,1)S(1)} collective-permute-done((bf16[192,8,128]{2,0,1:T(8,128)(2,1)S(1)}, bf16[192,8,128]{2,0,1:T(8,128)(2,1)S(1)}, u32[]{:S(2)}, u32[]{:S(2)}) %collective-permute-start.3) | collective-permute-done | bytes 393248 | tf_op jit(solution)/shard_map/ppermute | solution.py:19
  152.7 1.5 fusion.56
  154.3 5.7 %collective-permute-done.2 = bf16[192,8,128]{2,0,1:T(8,128)(2,1)S(1)} collective-permute-done((bf16[192,8,128]{2,0,1:T(8,128)(2,1)S(1)}, bf16[192,8,128]{2,0,1:T(8,128)(2,1)S(1)}, u32[]{:S(2)}, u32[]{:S(2)}) %collective-permute-start.2) | collective-permute-done | bytes 393248 | tf_op jit(solution)/shard_map/ppermute | solution.py:18
  160.0 1.5 fusion.53
  161.5 12.8 %concatenate.15 = f32[8,192,1536]{2,1,0:T(8,128)} concatenate(f32[8,192,192]{2,1,0:T(8,128)} %fusion.53, f32[8,192,192]{2,1,0:T(8,128)} %fusion.54, f32[8,192,192]{2,1,0:T(8,128)S(1)} %fusion.55, f32[8,192,192]{2,1,0:T(8,128)} %fusion.56, f32[8,192,192]{2,1,0:T(8,128)} %fusion.53, f32[8,192,192]{2,1,0:T(8,128)} %fusion.54, f32[8,192,192]{2,1,0:T(8,128)S(1)} %fusion.55, ...), dimensions={2} | concatenate | bytes 18874368 | tf_op jit(solution)/shard_map/jit(_roll_dynamic)/concatenate | solution.py:21
  174.3 4.5 %fusion = f32[8,192]{1,0:T(8,128)S(1)} fusion(f32[8,192,1536]{2,1,0:T(8,128)} %concatenate.15, s32[]{:T(128)S(6)} %select_n.42, pred[192,768]{1,0:T(8,128)(4,1)S(1)} %compare_and_fusion), kind=kLoop, calls=%fused_computation.5 | loop fusion | flops 3537408 | bytes 4872196 | tf_op jit(solution)/shard_map/reduce_sum | solution.py:121
  178.8 0.0 all-gather.3.cloned.1.call-done
  178.9 4.6 %fusion.23 = bf16[192,8,128]{2,0,1:T(8,128)(2,1)S(1)} fusion(bf16[768,1,8,128]{3,0,2,1:T(8,128)(2,1)} %all-gather.3.cloned.1.call-done, f32[8,192,1536]{2,1,0:T(8,128)} %concatenate.15, s32[]{:T(128)S(6)} %select_n.42, pred[192,768]{1,0:T(8,128)(4,1)S(1)} %compare_and_fusion, f32[192,8]{0,1:T(8,128)S(1)} %add_bitcast_fusion), kind=kOutput, calls=%fused_computation.22 | convolution fusion | flops 305922048 | bytes 6838276 | tf_op jit(solution)/shard_map/hqk,khd->qhd/dot_general | solution.py:122
  183.5 0.3 copy.11
  183.8 0.9 convert_element_type.66
  (30 shorter events, 0.2 us)
Async XLA Ops:
  6.5 82.9 %copy-start = (bf16[64,6144]{1,0:T(8,128)(2,1)S(1)}, bf16[64,6144]{1,0:T(8,128)(2,1)}, u32[]{:S(2)}) copy-start(bf16[64,6144]{1,0:T(8,128)(2,1)} %param.13) | copy-start | bytes 2359300
  6.5 4.7 %copy-start.2 = (bf16[3,512,512]{2,1,0:T(8,128)(2,1)S(1)}, bf16[3,512,512]{2,1,0:T(8,128)(2,1)}, u32[]{:S(2)}) copy-start(bf16[3,512,512]{2,1,0:T(8,128)(2,1)} %param.9) | copy-start | bytes 4718596
  6.5 5.1 %copy-start.6 = (bf16[512,16]{0,1:T(8,128)(2,1)S(1)}, bf16[512,16]{0,1:T(8,128)(2,1)}, u32[]{:S(2)}) copy-start(bf16[512,16]{0,1:T(8,128)(2,1)} %param.10) | copy-start | bytes 49156
  11.2 3.1 %copy-start.3 = (s32[2,128,1]{1,2,0:T(1,128)S(1)}, s32[2,128,1]{1,2,0:T(1,128)}, u32[]{:S(2)}) copy-start(s32[2,128,1]{1,2,0:T(1,128)} %param.11) | copy-start | bytes 3076
  11.2 3.6 %copy-start.4 = (s32[2,128]{1,0:T(2,128)S(1)}, s32[2,128]{1,0:T(2,128)}, u32[]{:S(2)}) copy-start(s32[2,128]{1,0:T(2,128)} %param.12) | copy-start | bytes 3076
  13.8 59.8 %collective-permute-start = (bf16[128,64]{1,0:T(8,128)(2,1)S(1)}, bf16[128,64]{1,0:T(8,128)(2,1)S(1)}, u32[]{:S(2)}, u32[]{:S(2)}) collective-permute-start(bf16[128,64]{1,0:T(8,128)(2,1)S(1)} %reshape_reshape.3), channel_id=1, source_target_pairs={{0,16},{16,0},{1,17},{17,1},{2,18},{18,2},{3,19},{19,3},{4,20},{20... | collective-permute-start | bytes 49160 | tf_op jit(solution)/shard_map/ppermute | solution.py:31
  16.5 55.9 %all-to-all-start.1 = ((s32[4,1,48]{2,1,0:T(1,128)}), s32[4,1,48]{2,1,0:T(1,128)S(1)}, u32[]{:S(2)}, u32[]{:S(2)}) async-start(s32[4,1,48]{2,1,0:T(1,128)} %all_to_all.10), calls=%async_computation.1 | async-start | bytes 4096 | tf_op jit(solution)/shard_map/all_to_all | solution.py:88
  22.4 48.7 %copy-start.7 = (u32[32]{0:T(128)S(1)}, u32[32]{0:T(128)}, u32[]{:S(2)}) copy-start(u32[32]{0:T(128)} %constant.103) | copy-start | bytes 388
  71.1 21.3 %copy-start.5 = (f32[6144]{0:T(1024)S(1)}, f32[6144]{0:T(1024)}, u32[]{:S(2)}) copy-start(f32[6144]{0:T(1024)} %param.14) | copy-start | bytes 73732
  75.2 14.1 %all-to-all-start = ((bf16[4,2,1536]{2,1,0:T(2,128)(2,1)}), bf16[4,2,1536]{2,1,0:T(2,128)(2,1)S(1)}, u32[]{:S(2)}, u32[]{:S(2)}) async-start(bf16[4,2,1536]{2,1,0:T(2,128)(2,1)} %reshape.205), calls=%async_computation | async-start | bytes 49152 | tf_op jit(solution)/shard_map/all_to_all | solution.py:87
  80.3 98.6 %all-gather.3.cloned.1.call-start = ((), (), s32[]{:S(2)}) async-start(), calls=%async_computation.2 | async-start | bytes 1966080 | tf_op jit(solution)/shard_map/all_gather | solution.py:105
  113.1 16.7 %collective-permute-start.1 = (bf16[192,8,128]{2,0,1:T(8,128)(2,1)S(1)}, bf16[192,8,128]{2,0,1:T(8,128)(2,1)S(1)}, u32[]{:S(2)}, u32[]{:S(2)}) collective-permute-start(bf16[192,8,128]{2,0,1:T(8,128)(2,1)S(1)} %get-tuple-element.7), channel_id=1, source_target_pairs={{0,4},{4,8},{8,12},{12,0},{1,5},{5,9},{9,13},{13,1},{2,6},{6,10},{... | collective-permute-start | bytes 1179656 | tf_op jit(solution)/shard_map/ppermute | solution.py:18
  114.8 37.9 %collective-permute-start.3 = (bf16[192,8,128]{2,0,1:T(8,128)(2,1)S(1)}, bf16[192,8,128]{2,0,1:T(8,128)(2,1)S(1)}, u32[]{:S(2)}, u32[]{:S(2)}) collective-permute-start(bf16[192,8,128]{2,0,1:T(8,128)(2,1)S(1)} %get-tuple-element.7), channel_id=1, source_target_pairs={{0,12},{4,0},{8,4},{12,8},{1,13},{5,1},{9,5},{13,9},{2,14},{6,2},{... | collective-permute-start | bytes 1179656 | tf_op jit(solution)/shard_map/ppermute | solution.py:19
  129.8 30.1 %collective-permute-start.2 = (bf16[192,8,128]{2,0,1:T(8,128)(2,1)S(1)}, bf16[192,8,128]{2,0,1:T(8,128)(2,1)S(1)}, u32[]{:S(2)}, u32[]{:S(2)}) collective-permute-start(bf16[192,8,128]{2,0,1:T(8,128)(2,1)S(1)} %collective-permute-done.1), channel_id=1, source_target_pairs={{0,4},{4,8},{8,12},{12,0},{1,5},{5,9},{9,13},{13,1},{2,6},{6,10},{... | collective-permute-start | bytes 1179656 | tf_op jit(solution)/shard_map/ppermute | solution.py:18
  178.8 5.9 %copy-start.1 = (bf16[64,6144]{1,0:T(8,128)(2,1)S(1)}, bf16[64,6144]{1,0:T(8,128)(2,1)}, u32[]{:S(2)}) copy-start(bf16[64,6144]{1,0:T(8,128)(2,1)} %param.13) | copy-start | bytes 2359300
Sparse Core Ops, SparseCore 0:
  112.7 52.6 all-gather.2
